TPU v7x, 512 devices: a whole 4x8x8 slice. The times are simulated.
512 devices in a mesh: row: 32 (over z, x_lo, core), col: 16 (over x_hi, y).
Axes of the slice: x: 4 (x_hi: 2, x_lo: 2; x = x_hi * 2 + x_lo), y: 8, z: 8, core: 2. Of those that a mesh axis runs over, the one named last changes fastest.
Arguments:
- slab_block: bfloat16 [65536, 2048], P('row', 'col'), may hold values from -6 to 6
- scale_first: bfloat16 [65536], P('row'), may hold values from 0.5 to 2
- scale_second: bfloat16 [65536], P('row'), may hold values from 0.5 to 2
- panel_lower: bfloat16 [65536, 4096], P('row', 'col'), may hold values from -0.09375 to 0.09375
Outputs:
- updated_slab: bfloat16 [65536, 2048], P('row', 'col')
All inputs are finite; a program needn't handle non-finite values.
Results may differ from a plain program's by a relative error of at most 0.015.
Values may be sent and summed in bfloat16 or wider, within the bound.
No kernel may reach another device: no remote copies, remote signals or barrier semaphores. Data moves between devices by JAX's collectives and lax.ppermute only.
A program may use at most 64 MiB of HBM per device.

v0:
```python
import jax
import jax.numpy as jnp
from jax import lax
from jax.sharding import PartitionSpec as P

PANEL_W = 4096
inv_root = 0.7071067811865476


def from_partner(block, axis, bit):
    count = lax.axis_size(axis)
    route = []
    for low in range(count):
        high = low | 1 << bit
        if high != low and high < count:
            route += [(low, high), (high, low)]
    return lax.ppermute(block, axis, route)


def per_device(slab_block, scale_first, scale_second, panel_lower):
    row_count, col_width = slab_block.shape
    groups = lax.axis_size("row")
    top_bit = groups.bit_length() - 1
    first = (scale_first.astype(jnp.float32)[:, None] * slab_block.astype(jnp.float32)).astype(
        jnp.bfloat16
    )
    my_index = lax.axis_index("row")
    partner = from_partner(first, "row", top_bit - 1)
    upper_one = my_index // (groups // 2) % 2 == 0
    own_vals = first.astype(jnp.float32)
    far_vals = partner.astype(jnp.float32)
    level_one = jnp.where(
        upper_one, (own_vals + far_vals) * inv_root, (far_vals - own_vals) * inv_root
    )
    second = (scale_second.astype(jnp.float32)[:, None] * level_one).astype(jnp.bfloat16)
    partner_two = from_partner(second, "row", top_bit - 2)
    upper_two = my_index // (groups // 4) % 2 == 0
    own_two = second.astype(jnp.float32)
    far_two = partner_two.astype(jnp.float32)
    level_two = jnp.where(upper_two, (own_two + far_two) * inv_root, (far_two - own_two) * inv_root)
    transformed = level_two.astype(jnp.bfloat16)
    moved = lax.all_to_all(
        transformed.reshape(row_count // groups, groups, col_width),
        "row",
        split_axis=1,
        concat_axis=0,
        tiled=True,
    )
    stored = moved.reshape(row_count, col_width)
    top_count = PANEL_W // groups
    top_local = stored[:top_count].reshape(top_count, 1, col_width)
    upper_rows = lax.all_gather(top_local, "row", axis=1, tiled=True).reshape(PANEL_W, col_width)
    block_width = panel_lower.shape[1]
    empty_sum = jnp.zeros((row_count, col_width), jnp.float32)
    shard_piece = lax.all_gather(panel_lower, "col", axis=1, tiled=True)
    blocks_in = shard_piece.shape[1] // block_width

    def one_block(blocknum, running):
        panel_part = lax.dynamic_slice_in_dim(shard_piece, blocknum * block_width, block_width, 1)
        rows_used = lax.dynamic_slice_in_dim(upper_rows, blocknum * block_width, block_width, 0)
        product = jnp.dot(panel_part, rows_used, preferred_element_type=jnp.float32)
        return running + product.astype(jnp.bfloat16).astype(jnp.float32)

    update_sum = lax.fori_loop(0, blocks_in, one_block, empty_sum)
    return (stored.astype(jnp.float32) - update_sum).astype(jnp.bfloat16)


def solution(mesh):
    placed = (P("row", "col"), P("row"), P("row"), P("row", "col"))
    return jax.shard_map(
        per_device, mesh=mesh, in_specs=placed, out_specs=P("row", "col"), check_vma=False
    )
```

profile of v0, /device:TPU:8, one launch (start us, length us, event | category | flops | bytes accessed | tf_op | source)
XLA Modules:
  0.0 444.3 jit_solution(17364804723847924911)
XLA Ops:
  6.5 0.0 all-gather.5.cloned.1.call-start
  6.5 0.7 convert_element_type.54
  7.2 1.4 multiply_convert_fusion
  8.6 10.9 %collective-permute-start = (bf16[2048,128]{1,0:T(8,128)(2,1)S(1)}, bf16[2048,128]{1,0:T(8,128)(2,1)S(1)}, u32[]{:S(2)}, u32[]{:S(2)}) collective-permute-start(bf16[2048,128]{1,0:T(8,128)(2,1)S(1)} %multiply_convert_fusion), channel_id=1, source_target_pairs={{0,256},{256,0},{16,272},{272,16},{32,288},{288,32},{48,304},{304,... | collective-permute-start | bytes 1572872 | tf_op jit(solution)/shard_map/ppermute | solution.py:17
  19.6 0.7 convert_element_type.53
  20.3 11.4 %collective-permute-done = bf16[2048,128]{1,0:T(8,128)(2,1)S(1)} collective-permute-done((bf16[2048,128]{1,0:T(8,128)(2,1)S(1)}, bf16[2048,128]{1,0:T(8,128)(2,1)S(1)}, u32[]{:S(2)}, u32[]{:S(2)}) %collective-permute-start) | collective-permute-done | bytes 524320 | tf_op jit(solution)/shard_map/ppermute | solution.py:17
  31.6 1.7 fusion.8
  33.3 15.4 %collective-permute-start.1 = (bf16[2048,128]{1,0:T(8,128)(2,1)S(1)}, bf16[2048,128]{1,0:T(8,128)(2,1)S(1)}, u32[]{:S(2)}, u32[]{:S(2)}) collective-permute-start(bf16[2048,128]{1,0:T(8,128)(2,1)S(1)} %fusion.8), channel_id=1, source_target_pairs={{0,128},{128,0},{16,144},{144,16},{32,160},{160,32},{48,176},{176,... | collective-permute-start | bytes 1572872 | tf_op jit(solution)/shard_map/ppermute | solution.py:17
  48.7 23.2 %collective-permute-done.1 = bf16[2048,128]{1,0:T(8,128)(2,1)S(1)} collective-permute-done((bf16[2048,128]{1,0:T(8,128)(2,1)S(1)}, bf16[2048,128]{1,0:T(8,128)(2,1)S(1)}, u32[]{:S(2)}, u32[]{:S(2)}) %collective-permute-start.1) | collective-permute-done | bytes 524320 | tf_op jit(solution)/shard_map/ppermute | solution.py:17
  72.0 0.3 fusion.12
  72.2 0.2 copy.8
  72.4 25.9 %all_to_all.15 = bf16[64,32,128]{2,0,1:T(8,128)(2,1)S(1)} all-to-all(bf16[64,32,128]{2,0,1:T(8,128)(2,1)S(1)} %copy.8), channel_id=1, replica_groups=mesh['row'=32,'col'=16] {'row'}, dimensions={1} | all-to-all | bytes 1048576 | tf_op jit(solution)/shard_map/all_to_all | solution.py:42
  98.3 0.6 slice.5
  99.0 0.0 all-gather.5.cloned.1.call-update
  99.0 0.0 all-gather.3.cloned.1.call-start
  99.0 0.7 all-gather.3.cloned.1.call-update
  99.7 62.5 %all-gather.5.cloned.1.call-done = bf16[128,32,128]{2,0,1:T(8,128)(2,1)} async-done(((bf16[128,1,128]{2,0,1:T(8,128)(2,1)}), bf16[128,32,128]{2,0,1:T(8,128)(2,1)}) %all-gather.5.cloned.1.call-update) | async-done | bytes 1048592 | tf_op jit(solution)/shard_map/all_gather | solution.py:52
  162.2 1.9 copy.9
  164.1 243.9 %all-gather.3.cloned.1.call-done = bf16[2048,4096]{1,0:T(8,128)(2,1)} async-done(((bf16[2048,256]{1,0:T(8,128)(2,1)}), bf16[2048,4096]{1,0:T(8,128)(2,1)}) %all-gather.3.cloned.1.call-update) | async-done | bytes 16777232 | tf_op jit(solution)/shard_map/all_gather | solution.py:55
  408.0 28.6 %while.14 = (s32[]{:T(128)}, f32[2048,128]{1,0:T(8,128)S(1)}, bf16[2048,4096]{1,0:T(8,128)(2,1)}, bf16[4096,128]{1,0:T(8,128)(2,1)S(1)}, s32[]{:T(128)}, /*index=5*/s32[]{:T(128)}, s32[]{:T(128)}, s32[]{:T(128)}) while((s32[]{:T(128)}, f32[2048,128]{1,0:T(8,128)S(1)}, bf16[2048,4096]{1,0:T(8,128)(2,1)}, ...), condition=%wide.region_1.2_spmd.clone, body=%wide.region_0.1_spmd.clone.sunk | while | flops 135266304 | bytes 3212948 | solution.py:64
  408.0 1.8 fusion.20
  409.8 1.8 fusion.20
  411.6 1.8 fusion.20
  413.3 1.8 fusion.20
  415.1 1.8 fusion.20
  416.9 1.8 fusion.20
  418.7 1.8 fusion.20
  420.5 1.8 fusion.20
  422.3 1.8 fusion.20
  424.1 1.8 fusion.20
  425.9 1.8 fusion.20
  427.6 1.8 fusion.20
  429.4 1.8 fusion.20
  431.2 1.8 fusion.20
  433.0 1.8 fusion.20
  434.8 1.8 fusion.20
  436.6 0.9 fusion.14
  (1 shorter events, 0.0 us)
Async XLA Ops:
  6.5 155.7 %all-gather.5.cloned.1.call-start = ((), (), s32[]{:S(2)}) async-start(), calls=%async_computation.2 | async-start | bytes 1081344 | tf_op jit(solution)/shard_map/all_gather | solution.py:52
  8.6 23.0 %collective-permute-start = (bf16[2048,128]{1,0:T(8,128)(2,1)S(1)}, bf16[2048,128]{1,0:T(8,128)(2,1)S(1)}, u32[]{:S(2)}, u32[]{:S(2)}) collective-permute-start(bf16[2048,128]{1,0:T(8,128)(2,1)S(1)} %multiply_convert_fusion), channel_id=1, source_target_pairs={{0,256},{256,0},{16,272},{272,16},{32,288},{288,32},{48,304},{304,... | collective-permute-start | bytes 1572872 | tf_op jit(solution)/shard_map/ppermute | solution.py:17
  33.3 38.7 %collective-permute-start.1 = (bf16[2048,128]{1,0:T(8,128)(2,1)S(1)}, bf16[2048,128]{1,0:T(8,128)(2,1)S(1)}, u32[]{:S(2)}, u32[]{:S(2)}) collective-permute-start(bf16[2048,128]{1,0:T(8,128)(2,1)S(1)} %fusion.8), channel_id=1, source_target_pairs={{0,128},{128,0},{16,144},{144,16},{32,160},{160,32},{48,176},{176,... | collective-permute-start | bytes 1572872 | tf_op jit(solution)/shard_map/ppermute | solution.py:17
  99.0 309.0 %all-gather.3.cloned.1.call-start = ((), (), s32[]{:S(2)}) async-start(), calls=%async_computation.1 | async-start | bytes 17825792 | tf_op jit(solution)/shard_map/all_gather | solution.py:55
Sparse Core Ops, SparseCore 0:
  99.1 63.0 all-gather.4
  165.3 242.6 all-gather.2
where the time goes:
time: 445 us; the launch traced here: 444 us
  waiting for transfers between devices  342 us (77%)
  matrix products  28.1 us (6%)
  starting transfers between devices  26.4 us (6%)
  blocking collectives  25.9 us (6%)
  between operations  13.5 us (3%)
  other arithmetic  5.61 us (1%)
    all_gather x1, waiting for transfers between devices, per_device(): shard_piece = lax.all_gather(panel_lower, 'col', axis=1, tiled=True)  244 us
    all_gather x1, waiting for transfers between devices, per_device(): lax.all_gather(top_local, 'row', axis=1, tiled=True)  62.5 us
    ppermute x2, waiting for transfers between devices, from_partner(): return lax.ppermute(block, axis, route)  34.6 us
    dot_general x16, matrix products, one_block(): product = jnp.dot(panel_part, rows_used, preferred_element_type=jnp.float32)  28.1 us
    ppermute x2, starting transfers between devices, from_partner(): return lax.ppermute(block, axis, route)  26.4 us
    all_to_all x1, blocking collectives, per_device(): lax.all_to_all(transformed.reshape(row_count // groups, groups, col_width...  25.9 us
  transfers between devices with their start and end apart: 4, of which 4 were waited for; matrix products, arithmetic and copies ran while one was open for 1% of the time, Pallas kernels for 0%

commit v1 on v0

--- a/solution.py
+++ b/solution.py
@@ -52,7 +52,9 @@
     upper_rows = lax.all_gather(top_local, "row", axis=1, tiled=True).reshape(PANEL_W, col_width)
     block_width = panel_lower.shape[1]
     empty_sum = jnp.zeros((row_count, col_width), jnp.float32)
-    shard_piece = lax.all_gather(panel_lower, "col", axis=1, tiled=True)
+    shard_piece = jnp.concatenate(
+        lax.all_to_all(jnp.stack([panel_lower] * lax.axis_size("col")), "col", 0, 0), axis=1
+    )
     blocks_in = shard_piece.shape[1] // block_width
 
     def one_block(blocknum, running):

time: 445 us -> 561 us (1.26)
  the two profiles are of different devices: /device:TPU:8 before, /device:TPU:37 now
where the time goes in v1:
time: 561 us; the launch traced here: 559 us
  waiting for transfers between devices  414 us (74%)
  starting transfers between devices  35.6 us (6%)
  matrix products  33.4 us (6%)
  local copies, waits for them, and re-layouts  31.2 us (6%)
  blocking collectives  24.9 us (4%)
  between operations  13.5 us (2%)
  other arithmetic  5.61 us (1%)
    all_to_all x1, waiting for transfers between devices, per_device(): lax.all_to_all(jnp.stack([panel_lower] * lax.axis_size('col')), 'col', 0, 0)  313 us
    all_gather x1, waiting for transfers between devices, per_device(): lax.all_gather(top_local, 'row', axis=1, tiled=True)  66.8 us
    ppermute x2, waiting for transfers between devices, from_partner(): return lax.ppermute(block, axis, route)  34.2 us
    dot_general x16, matrix products, one_block(): product = jnp.dot(panel_part, rows_used, preferred_element_type=jnp.float32)  33.4 us
    ppermute x2, starting transfers between devices, from_partner(): return lax.ppermute(block, axis, route)  26.5 us
    all_to_all x1, blocking collectives, per_device(): lax.all_to_all(transformed.reshape(row_count // groups, groups, col_width...  24.9 us
    all_to_all x1, local copies, waits for them, and re-layouts, per_device(): lax.all_to_all(jnp.stack([panel_lower] * lax.axis_size('col')), 'col', 0, 0)  21.7 us
  transfers between devices with their start and end apart: 4, of which 4 were waited for; matrix products, arithmetic and copies ran while one was open for 1% of the time, Pallas kernels for 0%

profile of v1, /device:TPU:37, one launch (start us, length us, event | category | flops | bytes accessed | tf_op | source)
XLA Modules:
  0.0 558.9 jit_solution(11976034694853730466)
XLA Ops:
  6.5 0.7 convert_element_type.54
  7.2 1.4 multiply_convert_fusion
  8.6 10.6 %collective-permute-start = (bf16[2048,128]{1,0:T(8,128)(2,1)S(1)}, bf16[2048,128]{1,0:T(8,128)(2,1)S(1)}, u32[]{:S(2)}, u32[]{:S(2)}) collective-permute-start(bf16[2048,128]{1,0:T(8,128)(2,1)S(1)} %multiply_convert_fusion), channel_id=1, source_target_pairs={{0,256},{256,0},{16,272},{272,16},{32,288},{288,32},{48,304},{304,... | collective-permute-start | bytes 1572872 | tf_op jit(solution)/shard_map/ppermute | solution.py:17
  19.3 0.7 convert_element_type.53
  20.0 11.0 %collective-permute-done = bf16[2048,128]{1,0:T(8,128)(2,1)S(1)} collective-permute-done((bf16[2048,128]{1,0:T(8,128)(2,1)S(1)}, bf16[2048,128]{1,0:T(8,128)(2,1)S(1)}, u32[]{:S(2)}, u32[]{:S(2)}) %collective-permute-start) | collective-permute-done | bytes 524320 | tf_op jit(solution)/shard_map/ppermute | solution.py:17
  31.0 1.7 fusion.8
  32.7 15.9 %collective-permute-start.1 = (bf16[2048,128]{1,0:T(8,128)(2,1)S(1)}, bf16[2048,128]{1,0:T(8,128)(2,1)S(1)}, u32[]{:S(2)}, u32[]{:S(2)}) collective-permute-start(bf16[2048,128]{1,0:T(8,128)(2,1)S(1)} %fusion.8), channel_id=1, source_target_pairs={{0,128},{128,0},{16,144},{144,16},{32,160},{160,32},{48,176},{176,... | collective-permute-start | bytes 1572872 | tf_op jit(solution)/shard_map/ppermute | solution.py:17
  48.6 23.2 %collective-permute-done.1 = bf16[2048,128]{1,0:T(8,128)(2,1)S(1)} collective-permute-done((bf16[2048,128]{1,0:T(8,128)(2,1)S(1)}, bf16[2048,128]{1,0:T(8,128)(2,1)S(1)}, u32[]{:S(2)}, u32[]{:S(2)}) %collective-permute-start.1) | collective-permute-done | bytes 524320 | tf_op jit(solution)/shard_map/ppermute | solution.py:17
  71.7 0.3 fusion.12
  72.0 0.2 copy.8
  72.2 24.9 %all_to_all.20 = bf16[64,32,128]{2,0,1:T(8,128)(2,1)S(1)} all-to-all(bf16[64,32,128]{2,0,1:T(8,128)(2,1)S(1)} %copy.8), channel_id=1, replica_groups=mesh['row'=32,'col'=16] {'row'}, dimensions={1} | all-to-all | bytes 1048576 | tf_op jit(solution)/shard_map/all_to_all | solution.py:42
  97.2 6.8 %stack.2 = bf16[16,2048,256]{2,1,0:T(8,128)(2,1)} broadcast(bf16[2048,256]{1,0:T(8,128)(2,1)} %param.9), dimensions={1,2} | broadcast | bytes 17825792 | tf_op jit(solution)/shard_map/stack | solution.py:56
  103.9 9.1 %all-to-all-start.1 = ((bf16[16,2048,256]{2,1,0:T(8,128)(2,1)}), bf16[16,2048,256]{2,1,0:T(8,128)(2,1)}, u32[]{:S(2)}, u32[]{:S(2)}) async-start(bf16[16,2048,256]{2,1,0:T(8,128)(2,1)} %stack.2), calls=%async_computation.1 | async-start | bytes 33554432 | tf_op jit(solution)/shard_map/all_to_all | solution.py:56
  113.0 0.0 all-gather.2.cloned.1.call-start
  113.1 0.6 slice.5
  113.7 0.1 all-gather.2.cloned.1.call-update
  113.8 66.8 %all-gather.2.cloned.1.call-done = bf16[128,32,128]{2,0,1:T(8,128)(2,1)} async-done(((bf16[128,1,128]{2,0,1:T(8,128)(2,1)}), bf16[128,32,128]{2,0,1:T(8,128)(2,1)}) %all-gather.2.cloned.1.call-update) | async-done | bytes 1048592 | tf_op jit(solution)/shard_map/all_gather | solution.py:52
  180.6 1.9 copy.10
  182.5 313.2 %all-to-all-done.1 = bf16[16,2048,256]{2,1,0:T(8,128)(2,1)} async-done(((bf16[16,2048,256]{2,1,0:T(8,128)(2,1)}), bf16[16,2048,256]{2,1,0:T(8,128)(2,1)}, u32[]{:S(2)}, u32[]{:S(2)}) %all-to-all-start.1) | async-done | bytes 16777248 | tf_op jit(solution)/shard_map/all_to_all | solution.py:56
  495.7 21.7 %copy.9 = bf16[16,2048,256]{1,2,0:T(8,128)(2,1)} copy(bf16[16,2048,256]{2,1,0:T(8,128)(2,1)} %all-to-all-done.1) | data formatting | bytes 33554432 | tf_op jit(solution)/shard_map/all_to_all | solution.py:56
  517.3 33.8 %while.14 = (s32[]{:T(128)}, f32[2048,128]{1,0:T(8,128)S(1)}, bf16[2048,4096]{0,1:T(8,128)(2,1)}, bf16[4096,128]{1,0:T(8,128)(2,1)S(1)}, s32[]{:T(128)}, /*index=5*/s32[]{:T(128)}, s32[]{:T(128)}, s32[]{:T(128)}) while((s32[]{:T(128)}, f32[2048,128]{1,0:T(8,128)S(1)}, bf16[2048,4096]{0,1:T(8,128)(2,1)}, ...), condition=%wide.region_1.2_spmd.clone, body=%wide.region_0.1_spmd.clone.sunk | while | flops 135266304 | bytes 3212948 | solution.py:66
  517.3 2.1 fusion.20
  519.5 2.1 fusion.20
  521.6 2.1 fusion.20
  523.7 2.1 fusion.20
  525.8 2.1 fusion.20
  527.9 2.1 fusion.20
  530.0 2.1 fusion.20
  532.1 2.1 fusion.20
  534.3 2.1 fusion.20
  536.4 2.1 fusion.20
  538.5 2.1 fusion.20
  540.6 2.1 fusion.20
  542.7 2.1 fusion.20
  544.8 2.1 fusion.20
  546.9 2.1 fusion.20
  549.1 2.1 fusion.20
  551.2 0.9 fusion.14
  (1 shorter events, 0.0 us)
Async XLA Ops:
  8.6 22.4 %collective-permute-start = (bf16[2048,128]{1,0:T(8,128)(2,1)S(1)}, bf16[2048,128]{1,0:T(8,128)(2,1)S(1)}, u32[]{:S(2)}, u32[]{:S(2)}) collective-permute-start(bf16[2048,128]{1,0:T(8,128)(2,1)S(1)} %multiply_convert_fusion), channel_id=1, source_target_pairs={{0,256},{256,0},{16,272},{272,16},{32,288},{288,32},{48,304},{304,... | collective-permute-start | bytes 1572872 | tf_op jit(solution)/shard_map/ppermute | solution.py:17
  32.7 39.1 %collective-permute-start.1 = (bf16[2048,128]{1,0:T(8,128)(2,1)S(1)}, bf16[2048,128]{1,0:T(8,128)(2,1)S(1)}, u32[]{:S(2)}, u32[]{:S(2)}) collective-permute-start(bf16[2048,128]{1,0:T(8,128)(2,1)S(1)} %fusion.8), channel_id=1, source_target_pairs={{0,128},{128,0},{16,144},{144,16},{32,160},{160,32},{48,176},{176,... | collective-permute-start | bytes 1572872 | tf_op jit(solution)/shard_map/ppermute | solution.py:17
  103.9 391.7 %all-to-all-start.1 = ((bf16[16,2048,256]{2,1,0:T(8,128)(2,1)}), bf16[16,2048,256]{2,1,0:T(8,128)(2,1)}, u32[]{:S(2)}, u32[]{:S(2)}) async-start(bf16[16,2048,256]{2,1,0:T(8,128)(2,1)} %stack.2), calls=%async_computation.1 | async-start | bytes 33554432 | tf_op jit(solution)/shard_map/all_to_all | solution.py:56
  113.0 67.6 %all-gather.2.cloned.1.call-start = ((), (), s32[]{:S(2)}) async-start(), calls=%async_computation.2 | async-start | bytes 1081344 | tf_op jit(solution)/shard_map/all_gather | solution.py:52
Sparse Core Ops, SparseCore 0:
  116.0 64.5 all-gather.1
